TPU v7x, 512 devices: a whole 4x8x8 slice. The times are simulated.
512 devices in a mesh: head: 8 (over z), tok: 64 (over x, y, core).
Axes of the slice: x: 4, y: 8, z: 8, core: 2. Of those that a mesh axis runs over, the one named last changes fastest.
Arguments:
- patches: bfloat16 [32768, 1280], P('tok')
- row_table: bfloat16 [64, 1280], replicated, may hold values from -0.59765625 to 0.59765625
- col_table: bfloat16 [64, 1280], replicated, may hold values from -0.59765625 to 0.59765625
- qkv_weight: bfloat16 [3, 1280, 1280], P(None, 'head'), may hold values from -0.15625 to 0.15625
- out_weight: bfloat16 [1280, 1280], P('head'), may hold values from -0.15625 to 0.15625
- merge_weight: bfloat16 [1280, 5120], P('head'), may hold values from -0.078125 to 0.078125
- segment_ids: int32 [32768], P('tok'), may hold values from 0 to 63, as said below
- image_grids: int32 [64, 2], replicated, may hold values from 2 to 62, as said below
- image_offsets: int32 [64], replicated, may hold values from 0 to 32736, as said below
- owners: int32 [64], replicated, may hold values from 0 to 63, each once
Outputs:
- delivered: bfloat16 [15872, 1280], P('tok', 'head')
Inputs may be any that keep to these rules, and one draw needn't show every extreme that they name: `segment_ids`: tokens of each image are consecutive and images follow in order; the pair p of token blocks (tokens 2 * p * 512 to 2 * (p + 1) * 512 - 1) holds exactly images 2 * p and 2 * p + 1, with no padding. `image_grids`: heights are even, widths are 16, and height times width is the image's token count. Within an image each 2x2 window of patches is four consecutive tokens (top left, top right, bottom left, bottom right), windows in row-major order. The longest image has exactly 992 tokens. `image_offsets`: the first token of each image, consistent with segment_ids. `owners`: every device index along tok owns exactly one image.
All inputs are finite; a program needn't handle non-finite values.
Results may differ from a plain program's by a relative error of at most 0.019.
Values may be sent and summed in bfloat16 or wider, within the bound.
No kernel may reach another device: no remote copies, remote signals or barrier semaphores. Data moves between devices by JAX's collectives and lax.ppermute only.
A program may use at most 64 MiB of HBM per device.

v0:
```python
import math
import jax
import jax.numpy as jnp
from jax import lax
from jax.sharding import PartitionSpec as P

HEAD_DIM = 80
CAP = 248


def partner(x, axis, apart):
    return lax.ppermute(x, axis, [(i, i ^ 1 << apart) for i in range(lax.axis_size(axis))])


def layer_norm(values):
    centered = values - jnp.mean(values, axis=-1, keepdims=True)
    variance = jnp.mean(centered * centered, axis=-1, keepdims=True)
    return centered * lax.rsqrt(variance + 1e-06)


def grid_place(token_pos, start_tok, width_now):
    local_pos = token_pos - start_tok
    window = local_pos // 4
    quarter = local_pos % 4
    half_width = jnp.maximum(width_now // 2, 1)
    row_index = 2 * (window // half_width) + quarter // 2
    col_index = 2 * (window % half_width) + quarter % 2
    return (row_index, col_index)


def dot_last(left, right):
    return lax.dot_general(
        left, right, (((1,), (1,)), ((), ())), preferred_element_type=jnp.float32
    )


def on_device(
    patches,
    row_table,
    col_table,
    qkv_weight,
    out_weight,
    merge_weight,
    segment_ids,
    image_grids,
    image_offsets,
    owners,
):
    full_weight = lax.all_gather(out_weight, "head", axis=0, tiled=True)
    block_rows = patches.shape[0]
    width_here = qkv_weight.shape[1]
    heads_here = width_here // HEAD_DIM
    image_count = owners.shape[0]
    image_ids = jnp.arange(image_count, dtype=jnp.int32)
    token_pos = lax.axis_index("tok") * block_rows + jnp.arange(block_rows, dtype=jnp.int32)
    member = segment_ids[:, None] == image_ids[None, :]
    start_tok = jnp.sum(jnp.where(member, image_offsets[None, :], 0), axis=1)
    width_now = jnp.sum(jnp.where(member, image_grids[None, :, 1], 0), axis=1)
    row_index, col_index = grid_place(token_pos, start_tok, width_now)
    side_ids = jnp.arange(row_table.shape[0], dtype=jnp.int32)
    row_onehot = (row_index[:, None] == side_ids[None, :]).astype(jnp.bfloat16)
    col_onehot = (col_index[:, None] == side_ids[None, :]).astype(jnp.bfloat16)
    resid = (
        patches.astype(jnp.float32)
        + jnp.dot(row_onehot, row_table, preferred_element_type=jnp.float32)
        + jnp.dot(col_onehot, col_table, preferred_element_type=jnp.float32)
    )
    normed = layer_norm(resid).astype(jnp.bfloat16)
    query_rows = dot_last(normed, qkv_weight[0]).astype(jnp.bfloat16)
    key_rows = dot_last(normed, qkv_weight[1]).astype(jnp.bfloat16)
    value_rows = dot_last(normed, qkv_weight[2]).astype(jnp.bfloat16)
    seg_wire = segment_ids.astype(jnp.bfloat16)
    far_keys, far_values, far_seg = partner((key_rows, value_rows, seg_wire), "tok", 0)
    query_heads = query_rows.reshape(block_rows, heads_here, HEAD_DIM)
    key_heads = jnp.concatenate([key_rows, far_keys], axis=0).reshape(
        2 * block_rows, heads_here, HEAD_DIM
    )
    value_heads = jnp.concatenate([value_rows, far_values], axis=0).reshape(
        2 * block_rows, heads_here, HEAD_DIM
    )
    query_seg = seg_wire.astype(jnp.float32)
    key_seg = jnp.concatenate([seg_wire, far_seg], axis=0).astype(jnp.float32)
    scores = jnp.einsum(
        "qhd,khd->hqk", query_heads, key_heads, preferred_element_type=jnp.float32
    ) * (1.0 / math.sqrt(HEAD_DIM))
    same_image = query_seg[:, None] == key_seg[None, :]
    raw_weights = jnp.where(same_image[None], jnp.exp(scores), 0.0)
    weight_sum = jnp.sum(raw_weights, axis=-1, keepdims=True)
    attn_probs = (raw_weights / weight_sum).astype(jnp.bfloat16)
    mixed = jnp.einsum("hqk,khd->qhd", attn_probs, value_heads, preferred_element_type=jnp.float32)
    attended = mixed.reshape(block_rows, width_here).astype(jnp.bfloat16)
    group = lax.axis_size("head")
    sent = jnp.broadcast_to(attended[None], (group,) + attended.shape)
    gathered = lax.all_to_all(sent, "head", 0, 0, tiled=True)
    head_total = jnp.einsum(
        "ztf,zfd->td",
        gathered,
        full_weight.reshape(group, width_here, -1),
        preferred_element_type=jnp.float32,
    )
    normed_two = layer_norm(resid + head_total).astype(jnp.bfloat16)
    merged = normed_two.reshape(block_rows // 4, 4 * normed_two.shape[1])
    projected = dot_last(merged, merge_weight).astype(jnp.bfloat16)
    places = lax.axis_size("tok")
    rows_here = projected.shape[0]
    share = rows_here // places
    spread = lax.all_to_all(projected.reshape(places, share, width_here), "tok", 0, 0, tiled=True)
    pair_ids = jnp.arange(places // 2, dtype=jnp.int32)
    place_ids = jnp.arange(places, dtype=jnp.int32)
    wanted = (owners.reshape(-1, 2)[None, :, :] == place_ids[:, None, None]).any(axis=2)
    pieces = jnp.dot(
        wanted.astype(jnp.bfloat16),
        spread.reshape(places // 2, 2 * share * width_here),
        preferred_element_type=jnp.float32,
    ).astype(jnp.bfloat16)
    pair_rows = lax.all_to_all(
        pieces.reshape(places, 2 * share, width_here), "tok", 0, 0, tiled=True
    ).reshape(2 * rows_here, width_here)
    owner_mask = owners == lax.axis_index("tok")
    image_id = jnp.sum(jnp.where(owner_mask, image_ids, 0))
    first_row = (
        jnp.sum(jnp.where(owner_mask, image_offsets, 0)) // 4 - image_id // 2 * 2 * rows_here
    )
    merged_count = jnp.sum(jnp.where(owner_mask, image_grids[:, 0] * image_grids[:, 1], 0)) // 4
    slot_ids = jnp.arange(CAP, dtype=jnp.int32)
    got_ids = jnp.arange(2 * rows_here, dtype=jnp.int32)
    row_of = got_ids // share % 2 * rows_here + got_ids // (2 * share) * share + got_ids % share
    slot_of = row_of - first_row
    selector = (slot_of[None, :] == slot_ids[:, None]) & (slot_ids < merged_count)[:, None]
    owner_rows = jnp.dot(
        selector.astype(jnp.bfloat16), pair_rows, preferred_element_type=jnp.float32
    )
    return owner_rows.astype(jnp.bfloat16)


def solution(mesh):
    placed = (
        P("tok", None),
        P(),
        P(),
        P(None, "head", None),
        P("head", None),
        P("head", None),
        P("tok"),
        P(),
        P(),
        P(),
    )
    return jax.shard_map(
        on_device, mesh=mesh, in_specs=placed, out_specs=P("tok", "head"), check_vma=False
    )
```

profile of v0, /device:TPU:1, one launch (start us, length us, event | category | flops | bytes accessed | tf_op | source)
XLA Modules:
  0.0 146.8 jit_solution(14957617930545872145)
XLA Ops:
  6.5 0.0 copy-start
  6.5 0.0 copy-start.2
  6.5 0.0 all-gather.2.cloned.1.call-start
  6.5 0.7 all-gather.2.cloned.1.call-update
  7.3 0.7 slice_bitcast_fusion
  7.9 0.8 select_reduce_fusion
  8.7 0.1 fusion.22
  8.9 2.0 %convolution_add_fusion.1 = f32[512,1280]{1,0:T(8,128)S(1)} fusion(bf16[64,1280]{1,0:T(8,128)(2,1)} %param.11, bf16[512,1280]{1,0:T(8,128)(2,1)} %param.10, s32[512]{0:T(512)S(1)} %get-tuple-element.13), kind=kOutput, calls=%fused_computation.3 | convolution fusion | flops 85229568 | bytes 4098048 | tf_op jit(solution)/shard_map/dot_general | solution.py:65
  10.9 0.0 copy-done.2
  10.9 0.6 fusion.41
  11.5 0.0 copy-start.1
  11.5 0.4 multiply_reduce_fusion.1
  11.9 0.0 copy-start.7
  11.9 0.0 copy-start.3
  12.0 0.3 multiply_convert_fusion.1
  12.3 0.8 copy-done.1
  13.0 0.7 copy-done.7
  13.7 0.6 convolution_convert_fusion
  14.3 8.8 %collective-permute-start.2 = (bf16[512,160]{0,1:T(8,128)(2,1)S(1)}, bf16[512,160]{0,1:T(8,128)(2,1)S(1)}, u32[]{:S(2)}, u32[]{:S(2)}) collective-permute-start(bf16[512,160]{0,1:T(8,128)(2,1)S(1)} %convolution_convert_fusion), channel_id=1, source_target_pairs={{0,1},{1,0},{2,3},{3,2},{4,5},{5,4},{6,7},{7,6},{8,9},{9,8},{10,11... | collective-permute-start | bytes 491528 | tf_op jit(solution)/shard_map/ppermute | solution.py:12
  23.1 0.0 copy-done.3
  23.1 1.9 %collective-permute-start.1 = (bf16[512]{0:T(512)(128)(2,1)S(1)}, bf16[512]{0:T(512)(128)(2,1)S(1)}, u32[]{:S(2)}, u32[]{:S(2)}) collective-permute-start(bf16[512]{0:T(512)(128)(2,1)S(1)} %get-tuple-element.11), channel_id=1, source_target_pairs={{0,1},{1,0},{2,3},{3,2},{4,5},{5,4},{6,7},{7,6},{8,9},{9,8},{10,11... | collective-permute-start | bytes 3080 | tf_op jit(solution)/shard_map/ppermute | solution.py:12
  25.0 0.6 convolution_convert_fusion.2
  25.6 2.4 %collective-permute-start = (bf16[512,160]{0,1:T(8,128)(2,1)S(1)}, bf16[512,160]{0,1:T(8,128)(2,1)S(1)}, u32[]{:S(2)}, u32[]{:S(2)}) collective-permute-start(bf16[512,160]{0,1:T(8,128)(2,1)S(1)} %convolution_convert_fusion.2), channel_id=1, source_target_pairs={{0,1},{1,0},{2,3},{3,2},{4,5},{5,4},{6,7},{7,6},{8,9},{9,8},{10,11... | collective-permute-start | bytes 491528 | tf_op jit(solution)/shard_map/ppermute | solution.py:12
  28.0 0.6 convolution_convert_fusion.1
  28.6 0.0 collective-permute-done.1
  28.6 0.4 broadcast_compare_fusion
  29.0 0.0 collective-permute-done.2
  29.1 0.0 collective-permute-done
  29.1 1.5 %fusion = (f32[2,512]{1,0:T(2,128)S(1)}, f32[2,512,1024]{2,1,0:T(8,128)S(1)}) fusion(pred[512,1024]{1,0:T(8,128)(4,1)S(1)} %broadcast_compare_fusion, bf16[512,2,80]{0,2,1:T(8,128)(2,1)S(1)} %bitcast.49, bf16[1024,2,80]{0,2,1:T(8,128)(2,1)S(1)} %bitcast.46), kind=kOutput, calls=%fused_computation.4 | convolution fusion | flops 170916864 | bytes 5214208 | tf_op jit(solution)/shard_map/qhd,khd->hqk/dot_general | solution.py:83
  30.6 1.4 fusion.3
  31.9 0.0 copy-start.5
  32.0 0.0 copy-start.4
  32.0 0.0 copy-start.6
  32.0 1.2 broadcast_in_dim.69
  33.2 4.7 %all-to-all-start = ((bf16[8,512,160]{1,2,0:T(8,128)(2,1)}), bf16[8,512,160]{1,2,0:T(8,128)(2,1)S(1)}, u32[]{:S(2)}, u32[]{:S(2)}) async-start(bf16[8,512,160]{1,2,0:T(8,128)(2,1)} %broadcast_in_dim.69), calls=%async_computation | async-start | bytes 2621440 | tf_op jit(solution)/shard_map/all_to_all | solution.py:94
  37.8 0.0 copy-done.5
  37.8 0.1 eq.109
  37.9 0.0 copy-done.4
  38.0 0.0 copy-done.6
  38.0 0.7 fusion.37
  40.0 0.1 copy.12
  41.4 44.9 %all-to-all-done = bf16[8,512,160]{1,2,0:T(8,128)(2,1)S(1)} async-done(((bf16[8,512,160]{1,2,0:T(8,128)(2,1)}), bf16[8,512,160]{1,2,0:T(8,128)(2,1)S(1)}, u32[]{:S(2)}, u32[]{:S(2)}) %all-to-all-start) | async-done | bytes 1310752 | tf_op jit(solution)/shard_map/all_to_all | solution.py:94
  86.3 6.4 %all-gather.2.cloned.1.call-done = bf16[1280,1280]{1,0:T(8,128)(2,1)} async-done(((bf16[160,1280]{1,0:T(8,128)(2,1)}), bf16[1280,1280]{1,0:T(8,128)(2,1)}) %all-gather.2.cloned.1.call-update) | async-done | bytes 3276816 | tf_op jit(solution)/shard_map/all_gather | solution.py:49
  92.7 4.8 %fusion.42 = (f32[512]{0:T(512)S(1)}, f32[512,1280]{1,0:T(8,128)S(1)}) fusion(f32[512,1280]{1,0:T(8,128)} %copy-done.1, bf16[8,512,160]{1,2,0:T(8,128)(2,1)S(1)} %all-to-all-done, bf16[8,160,1280]{2,1,0:T(8,128)(2,1)} %bitcast.45), kind=kOutput, calls=%fused_computation.113 | convolution fusion | flops 1679031808 | bytes 9832448 | tf_op jit(solution)/shard_map/ztf,zfd->td/dot_general | solution.py:95
  97.5 0.4 multiply_reduce_fusion
  98.0 0.3 multiply_convert_fusion
  98.3 1.7 %reshape.260 = bf16[128,5120]{1,0:T(8,128)(2,1)} reshape(bf16[512,1280]{1,0:T(8,128)(2,1)S(1)} %multiply_convert_fusion) | data formatting | bytes 2621440 | tf_op jit(solution)/shard_map/reshape | solution.py:102
  100.0 0.0 copy-done
  100.0 1.9 %convolution_convert_fusion.5 = bf16[128,160]{0,1:T(8,128)(2,1)S(1)} fusion(bf16[128,5120]{1,0:T(8,128)(2,1)} %reshape.260, bf16[160,5120]{1,0:T(8,128)(2,1)S(1)} %copy-done), kind=kOutput, calls=%fused_computation.18 | convolution fusion | flops 209735680 | bytes 2990080 | tf_op jit(solution)/shard_map/dot_general | solution.py:32
  101.9 0.1 copy.13
  102.0 0.7 reshape.261
  102.7 10.4 %all-to-all-start.1 = ((bf16[64,2,160]{2,1,0:T(2,128)(2,1)}), bf16[64,2,160]{2,1,0:T(2,128)(2,1)S(1)}, u32[]{:S(2)}, u32[]{:S(2)}) async-start(bf16[64,2,160]{2,1,0:T(2,128)(2,1)} %reshape.261), calls=%async_computation.1 | async-start | bytes 131072 | tf_op jit(solution)/shard_map/all_to_all | solution.py:107
  113.1 0.1 fusion.16
  113.2 9.7 %all-to-all-done.1 = bf16[64,2,160]{2,1,0:T(2,128)(2,1)S(1)} async-done(((bf16[64,2,160]{2,1,0:T(2,128)(2,1)}), bf16[64,2,160]{2,1,0:T(2,128)(2,1)S(1)}, u32[]{:S(2)}, u32[]{:S(2)}) %all-to-all-start.1) | async-done | bytes 40992 | tf_op jit(solution)/shard_map/all_to_all | solution.py:107
  122.9 0.1 reshape.262
  123.0 0.2 convolution_convert_fusion.4
  123.2 0.8 reshape.263
  124.0 4.4 %all-to-all-start.2 = ((bf16[64,4,160]{2,1,0:T(4,128)(2,1)}), bf16[64,4,160]{2,1,0:T(4,128)(2,1)S(1)}, u32[]{:S(2)}, u32[]{:S(2)}) async-start(bf16[64,4,160]{2,1,0:T(4,128)(2,1)} %reshape.263), calls=%async_computation.2 | async-start | bytes 262144 | tf_op jit(solution)/shard_map/all_to_all | solution.py:116
  133.4 5.5 %all-to-all-done.2 = bf16[64,4,160]{2,1,0:T(4,128)(2,1)S(1)} async-done(((bf16[64,4,160]{2,1,0:T(4,128)(2,1)}), bf16[64,4,160]{2,1,0:T(4,128)(2,1)S(1)}, u32[]{:S(2)}, u32[]{:S(2)}) %all-to-all-start.2) | async-done | bytes 81952 | tf_op jit(solution)/shard_map/all_to_all | solution.py:116
  138.9 0.1 reshape.264
  139.0 0.9 convolution_convert_fusion.3
  (10 shorter events, 0.1 us)
Async XLA Ops:
  6.5 93.4 %copy-start = (bf16[160,5120]{1,0:T(8,128)(2,1)S(1)}, bf16[160,5120]{1,0:T(8,128)(2,1)}, u32[]{:S(2)}) copy-start(bf16[160,5120]{1,0:T(8,128)(2,1)} %param.15) | copy-start | bytes 4915204
  6.5 4.3 %copy-start.2 = (bf16[64,1280]{1,0:T(8,128)(2,1)S(1)}, bf16[64,1280]{1,0:T(8,128)(2,1)}, u32[]{:S(2)}) copy-start(bf16[64,1280]{1,0:T(8,128)(2,1)} %param.12) | copy-start | bytes 491524
  6.5 86.2 %all-gather.2.cloned.1.call-start = ((), (), s32[]{:S(2)}) async-start(), calls=%async_computation.3 | async-start | bytes 3686400 | tf_op jit(solution)/shard_map/all_gather | solution.py:49
  11.5 1.5 %copy-start.1 = (f32[512,1280]{1,0:T(8,128)}, f32[512,1280]{1,0:T(8,128)S(1)}, u32[]{:S(2)}) copy-start(f32[512,1280]{1,0:T(8,128)S(1)} %get-tuple-element.15) | copy-start | bytes 7864324
  11.9 1.8 %copy-start.7 = (bf16[3,160,1280]{2,1,0:T(8,128)(2,1)S(1)}, bf16[3,160,1280]{2,1,0:T(8,128)(2,1)}, u32[]{:S(2)}) copy-start(bf16[3,160,1280]{2,1,0:T(8,128)(2,1)} %param.13) | copy-start | bytes 3686404
  11.9 11.2 %copy-start.3 = (s32[512]{0:T(512)S(1)}, s32[512]{0:T(512)}, u32[]{:S(2)}) copy-start(s32[512]{0:T(512)} %param.16) | copy-start | bytes 6148
  14.3 14.7 %collective-permute-start.2 = (bf16[512,160]{0,1:T(8,128)(2,1)S(1)}, bf16[512,160]{0,1:T(8,128)(2,1)S(1)}, u32[]{:S(2)}, u32[]{:S(2)}) collective-permute-start(bf16[512,160]{0,1:T(8,128)(2,1)S(1)} %convolution_convert_fusion), channel_id=1, source_target_pairs={{0,1},{1,0},{2,3},{3,2},{4,5},{5,4},{6,7},{7,6},{8,9},{9,8},{10,11... | collective-permute-start | bytes 491528 | tf_op jit(solution)/shard_map/ppermute | solution.py:12
  23.1 5.5 %collective-permute-start.1 = (bf16[512]{0:T(512)(128)(2,1)S(1)}, bf16[512]{0:T(512)(128)(2,1)S(1)}, u32[]{:S(2)}, u32[]{:S(2)}) collective-permute-start(bf16[512]{0:T(512)(128)(2,1)S(1)} %get-tuple-element.11), channel_id=1, source_target_pairs={{0,1},{1,0},{2,3},{3,2},{4,5},{5,4},{6,7},{7,6},{8,9},{9,8},{10,11... | collective-permute-start | bytes 3080 | tf_op jit(solution)/shard_map/ppermute | solution.py:12
  25.6 3.4 %collective-permute-start = (bf16[512,160]{0,1:T(8,128)(2,1)S(1)}, bf16[512,160]{0,1:T(8,128)(2,1)S(1)}, u32[]{:S(2)}, u32[]{:S(2)}) collective-permute-start(bf16[512,160]{0,1:T(8,128)(2,1)S(1)} %convolution_convert_fusion.2), channel_id=1, source_target_pairs={{0,1},{1,0},{2,3},{3,2},{4,5},{5,4},{6,7},{7,6},{8,9},{9,8},{10,11... | collective-permute-start | bytes 491528 | tf_op jit(solution)/shard_map/ppermute | solution.py:12
  31.9 5.9 %copy-start.5 = (s32[64]{0:T(128)S(1)}, s32[64]{0:T(128)}, u32[]{:S(2)}) copy-start(s32[64]{0:T(128)} %param.19) | copy-start | bytes 772
  32.0 6.0 %copy-start.4 = (s32[64]{0:T(128)S(1)}, s32[64]{0:T(128)}, u32[]{:S(2)}) copy-start(s32[64]{0:T(128)} %param.18) | copy-start | bytes 772
  32.0 6.0 %copy-start.6 = (s32[64,2]{0,1:T(2,128)S(1)}, s32[64,2]{0,1:T(2,128)}, u32[]{:S(2)}) copy-start(s32[64,2]{0,1:T(2,128)} %param.17) | copy-start | bytes 1540
  33.2 53.2 %all-to-all-start = ((bf16[8,512,160]{1,2,0:T(8,128)(2,1)}), bf16[8,512,160]{1,2,0:T(8,128)(2,1)S(1)}, u32[]{:S(2)}, u32[]{:S(2)}) async-start(bf16[8,512,160]{1,2,0:T(8,128)(2,1)} %broadcast_in_dim.69), calls=%async_computation | async-start | bytes 2621440 | tf_op jit(solution)/shard_map/all_to_all | solution.py:94
  102.7 20.2 %all-to-all-start.1 = ((bf16[64,2,160]{2,1,0:T(2,128)(2,1)}), bf16[64,2,160]{2,1,0:T(2,128)(2,1)S(1)}, u32[]{:S(2)}, u32[]{:S(2)}) async-start(bf16[64,2,160]{2,1,0:T(2,128)(2,1)} %reshape.261), calls=%async_computation.1 | async-start | bytes 131072 | tf_op jit(solution)/shard_map/all_to_all | solution.py:107
  124.0 14.9 %all-to-all-start.2 = ((bf16[64,4,160]{2,1,0:T(4,128)(2,1)}), bf16[64,4,160]{2,1,0:T(4,128)(2,1)S(1)}, u32[]{:S(2)}, u32[]{:S(2)}) async-start(bf16[64,4,160]{2,1,0:T(4,128)(2,1)} %reshape.263), calls=%async_computation.2 | async-start | bytes 262144 | tf_op jit(solution)/shard_map/all_to_all | solution.py:116
Sparse Core Ops, SparseCore 0:
  9.4 83.2 all-gather.1
where the time goes:
time: 147 us
  waiting for transfers between devices  67.3 us (46%)
  starting transfers between devices  32.6 us (22%)
  between operations  21.2 us (14%)
  matrix products  15.1 us (10%)
  local copies, waits for them, and re-layouts  6.95 us (5%)
  other arithmetic  3.64 us (2%)
    all_to_all x1, waiting for transfers between devices, on_device(): gathered = lax.all_to_all(sent, 'head', 0, 0, tiled=True)  44.9 us
    ppermute x3, starting transfers between devices, partner(): lax.ppermute(x, axis, [(i, i ^ 1 << apart) for i in range(lax.axis_size(a...  13.1 us
    all_to_all x1, starting transfers between devices, on_device(): lax.all_to_all(projected.reshape(places, share, width_here), 'tok', 0, 0,...  10.4 us
    all_to_all x1, waiting for transfers between devices, on_device(): lax.all_to_all(projected.reshape(places, share, width_here), 'tok', 0, 0,...  9.7 us
    all_gather x1, waiting for transfers between devices, on_device(): full_weight = lax.all_gather(out_weight, 'head', axis=0, tiled=True)  6.37 us
    all_to_all x1, waiting for transfers between devices, on_device(): lax.all_to_all(pieces.reshape(places, 2 * share, width_here), 'tok', 0, 0...  5.53 us
    dot_general x1, matrix products, on_device(): jnp.einsum('ztf,zfd->td', gathered, full_weight.reshape(group, width_here...  4.83 us
    all_to_all x1, starting transfers between devices, on_device(): gathered = lax.all_to_all(sent, 'head', 0, 0, tiled=True)  4.66 us
  transfers between devices with their start and end apart: 7, of which 4 were waited for; matrix products, arithmetic and copies ran while one was open for 8% of the time, Pallas kernels for 0%

commit v1 on v0

--- a/solution.py
+++ b/solution.py
@@ -6,6 +6,19 @@
 
 HEAD_DIM = 80
 CAP = 248
+
+
+def ring_gather(x, axis, dim):
+    ways = lax.axis_size(axis)
+    up = [(d, (d + 1) % ways) for d in range(ways)]
+    down = [(d, (d - 1) % ways) for d in range(ways)]
+    earlier, later = ([x], [x])
+    for _ in range(ways // 2):
+        earlier.append(lax.ppermute(earlier[-1], axis, up))
+    for _ in range((ways - 1) // 2):
+        later.append(lax.ppermute(later[-1], axis, down))
+    line = jnp.concatenate([*earlier[::-1], *later[1:]], axis=dim)
+    return jnp.roll(line, (lax.axis_index(axis) - ways // 2) * x.shape[dim], axis=dim)
 
 
 def partner(x, axis, apart):
@@ -46,7 +59,7 @@
     image_offsets,
     owners,
 ):
-    full_weight = lax.all_gather(out_weight, "head", axis=0, tiled=True)
+    full_weight = ring_gather(out_weight, "head", 0)
     block_rows = patches.shape[0]
     width_here = qkv_weight.shape[1]
     heads_here = width_here // HEAD_DIM

time: 147 us -> 168 us (1.14)
  starting transfers between devices: 32.6 us -> 58.1 us
  local copies, waits for them, and re-layouts: 6.95 us -> 20 us
  between operations: 21.2 us -> 8.17 us
  waiting for transfers between devices: 67.3 us -> 54.7 us
  other arithmetic: 3.64 us -> 6.96 us
  matrix products: 15.1 us -> 18.3 us
    all_to_all x1, waiting for transfers between devices: 44.9 us -> 0.01 us  [on_device(): gathered = lax.all_to_all(sent, 'head', 0, 0, tiled=True)]
    ppermute x0 -> x7, waiting for transfers between devices: none -> 39.6 us  [the longest x3 25.9 us: ring_gather(): later.append(lax.ppermute(later[-1], axis, down))]
    ppermute x0 -> x7, starting transfers between devices: none -> 28.6 us  [the longest x3 17.9 us: ring_gather(): later.append(lax.ppermute(later[-1], axis, down))]
    unnamed x16 -> x39, local copies, waits for them, and re-layouts: 1.49 us -> 12.1 us
    all_gather x1 -> x0, waiting for transfers between devices: 6.37 us -> none  [on_device(): full_weight = lax.all_gather(out_weight, 'head', axis=0, tiled=True)]
    ppermute x3, starting transfers between devices: 13.1 us -> 7.19 us  [partner(): lax.ppermute(x, axis, [(i, i ^ 1 << apart) for i in range(lax.axis_size(a...]
    all_to_all x1, starting transfers between devices: 10.4 us -> 13.3 us  [on_device(): lax.all_to_all(projected.reshape(places, share, width_here), 'tok', 0, 0,...]
    dynamic_slice x0 -> x1, local copies, waits for them, and re-layouts: none -> 2.45 us  [ring_gather(): jnp.roll(line, (lax.axis_index(axis) - ways // 2) * x.shape[dim], axis=dim)]
  transfers between devices with their start and end apart: 7 -> 13, of which waited for: 4 -> 5; matrix products, arithmetic and copies ran while one was open for 8% -> 19% of each run, Pallas kernels for 0% -> 0%
where the time goes in v1:
time: 168 us; the launch traced here: 166 us
  starting transfers between devices  58.1 us (35%)
  waiting for transfers between devices  54.7 us (33%)
  local copies, waits for them, and re-layouts  20 us (12%)
  matrix products  18.3 us (11%)
  between operations  8.17 us (5%)
  other arithmetic  6.96 us (4%)
    ppermute x3, waiting for transfers between devices, ring_gather(): later.append(lax.ppermute(later[-1], axis, down))  25.9 us
    ppermute x3, starting transfers between devices, ring_gather(): later.append(lax.ppermute(later[-1], axis, down))  17.9 us
    ppermute x4, waiting for transfers between devices, ring_gather(): earlier.append(lax.ppermute(earlier[-1], axis, up))  13.7 us
    all_to_all x1, starting transfers between devices, on_device(): lax.all_to_all(projected.reshape(places, share, width_here), 'tok', 0, 0,...  13.3 us
    unnamed x39, local copies, waits for them, and re-layouts  12.1 us
    ppermute x4, starting transfers between devices, ring_gather(): earlier.append(lax.ppermute(earlier[-1], axis, up))  10.7 us
    all_to_all x1, waiting for transfers between devices, on_device(): lax.all_to_all(projected.reshape(places, share, width_here), 'tok', 0, 0,...  9.7 us
    ppermute x3, starting transfers between devices, partner(): lax.ppermute(x, axis, [(i, i ^ 1 << apart) for i in range(lax.axis_size(a...  7.19 us
  transfers between devices with their start and end apart: 13, of which 5 were waited for; matrix products, arithmetic and copies ran while one was open for 19% of the time, Pallas kernels for 0%

profile of v1, /device:TPU:1, one launch (start us, length us, event | category | flops | bytes accessed | tf_op | source)
XLA Modules:
  0.0 166.3 jit_solution(16285843154467064014)
XLA Ops:
  0.0 5.0 %collective-permute-start.3 = (bf16[160,1280]{1,0:T(8,128)(2,1)}, bf16[160,1280]{1,0:T(8,128)(2,1)S(1)}, u32[]{:S(2)}, u32[]{:S(2)}) collective-permute-start(bf16[160,1280]{1,0:T(8,128)(2,1)} %param.14), channel_id=1, source_target_pairs={{0,64},{64,128},{128,192},{192,256},{256,320},{320,384},{384,448},... | collective-permute-start | bytes 1228808 | tf_op jit(solution)/shard_map/ppermute | solution.py:17
  5.0 8.6 %collective-permute-start.7 = (bf16[160,1280]{1,0:T(8,128)(2,1)}, bf16[160,1280]{1,0:T(8,128)(2,1)}, u32[]{:S(2)}, u32[]{:S(2)}) collective-permute-start(bf16[160,1280]{1,0:T(8,128)(2,1)} %param.14), channel_id=1, source_target_pairs={{0,448},{64,0},{128,64},{192,128},{256,192},{320,256},{384,320},{4... | collective-permute-start | bytes 1228808 | tf_op jit(solution)/shard_map/ppermute | solution.py:19
  13.6 0.7 slice_bitcast_fusion
  14.3 0.8 select_reduce_fusion
  15.0 0.1 fusion.22
  15.2 2.0 %convolution_add_fusion.1 = f32[512,1280]{1,0:T(8,128)S(1)} fusion(bf16[64,1280]{1,0:T(8,128)(2,1)} %param.11, bf16[512,1280]{1,0:T(8,128)(2,1)} %param.10, s32[512]{0:T(512)S(1)} %get-tuple-element.13), kind=kOutput, calls=%fused_computation.3 | convolution fusion | flops 85229568 | bytes 4098048 | tf_op jit(solution)/shard_map/dot_general | solution.py:78
  17.2 0.6 fusion.41
  17.8 0.4 multiply_reduce_fusion.1
  18.3 0.3 multiply_convert_fusion.1
  18.6 0.7 copy-done.1
  19.3 0.7 copy-done.11
  20.0 1.2 convolution_convert_fusion
  21.3 2.9 %collective-permute-start.2 = (bf16[512,160]{0,1:T(8,128)(2,1)}, bf16[512,160]{0,1:T(8,128)(2,1)}, u32[]{:S(2)}, u32[]{:S(2)}) collective-permute-start(bf16[512,160]{0,1:T(8,128)(2,1)} %convolution_convert_fusion), channel_id=1, source_target_pairs={{0,1},{1,0},{2,3},{3,2},{4,5},{5,4},{6,7},{7,6},{8,9},{9,8},{10,11... | collective-permute-start | bytes 491528 | tf_op jit(solution)/shard_map/ppermute | solution.py:25
  24.2 1.9 %collective-permute-start.1 = (bf16[512]{0:T(512)(128)(2,1)S(1)}, bf16[512]{0:T(512)(128)(2,1)}, u32[]{:S(2)}, u32[]{:S(2)}) collective-permute-start(bf16[512]{0:T(512)(128)(2,1)S(1)} %get-tuple-element.11), channel_id=1, source_target_pairs={{0,1},{1,0},{2,3},{3,2},{4,5},{5,4},{6,7},{7,6},{8,9},{9,8},{10,11... | collective-permute-start | bytes 3080 | tf_op jit(solution)/shard_map/ppermute | solution.py:25
  26.1 0.6 convolution_convert_fusion.2
  26.7 2.4 %collective-permute-start = (bf16[512,160]{0,1:T(8,128)(2,1)S(1)}, bf16[512,160]{0,1:T(8,128)(2,1)}, u32[]{:S(2)}, u32[]{:S(2)}) collective-permute-start(bf16[512,160]{0,1:T(8,128)(2,1)S(1)} %convolution_convert_fusion.2), channel_id=1, source_target_pairs={{0,1},{1,0},{2,3},{3,2},{4,5},{5,4},{6,7},{7,6},{8,9},{9,8},{10,11... | collective-permute-start | bytes 491528 | tf_op jit(solution)/shard_map/ppermute | solution.py:25
  29.1 0.1 eq.112
  29.2 1.5 fusion.37
  32.7 2.2 %convolution_convert_fusion.1 = bf16[512,160]{0,1:T(8,128)(2,1)} fusion(bf16[512,1280]{1,0:T(8,128)(2,1)S(1)} %multiply_convert_fusion.1, bf16[3,160,1280]{2,1,0:T(8,128)(2,1)} %param.13), kind=kOutput, calls=%fused_computation.14 | convolution fusion | flops 209797120 | bytes 1884160 | tf_op jit(solution)/shard_map/dot_general | solution.py:45
  34.9 0.1 copy.12
  35.7 1.9 %collective-permute-start.4 = (bf16[160,1280]{1,0:T(8,128)(2,1)S(1)}, bf16[160,1280]{1,0:T(8,128)(2,1)S(1)}, u32[]{:S(2)}, u32[]{:S(2)}) collective-permute-start(bf16[160,1280]{1,0:T(8,128)(2,1)S(1)} %collective-permute-done.3), channel_id=1, source_target_pairs={{0,64},{64,128},{128,192},{192,256},{256,320},{320,384},{384,448},... | collective-permute-start | bytes 1228808 | tf_op jit(solution)/shard_map/ppermute | solution.py:17
  37.6 0.7 maximum_convert_fusion
  38.3 0.4 broadcast_compare_fusion
  38.7 1.0 pad_maximum_fusion.1
  39.7 10.2 %collective-permute-done.4 = bf16[160,1280]{1,0:T(8,128)(2,1)S(1)} collective-permute-done((bf16[160,1280]{1,0:T(8,128)(2,1)S(1)}, bf16[160,1280]{1,0:T(8,128)(2,1)S(1)}, u32[]{:S(2)}, u32[]{:S(2)}) %collective-permute-start.4) | collective-permute-done | bytes 409632 | tf_op jit(solution)/shard_map/ppermute | solution.py:17
  49.9 1.9 %collective-permute-start.5 = (bf16[160,1280]{1,0:T(8,128)(2,1)S(1)}, bf16[160,1280]{1,0:T(8,128)(2,1)}, u32[]{:S(2)}, u32[]{:S(2)}) collective-permute-start(bf16[160,1280]{1,0:T(8,128)(2,1)S(1)} %collective-permute-done.4), channel_id=1, source_target_pairs={{0,64},{64,128},{128,192},{192,256},{256,320},{320,384},{384,448},... | collective-permute-start | bytes 1228808 | tf_op jit(solution)/shard_map/ppermute | solution.py:17
  51.8 0.9 pad_maximum_fusion
  52.8 2.4 %fusion = (f32[2,512]{1,0:T(2,128)S(1)}, f32[2,512,1024]{2,1,0:T(8,128)S(1)}) fusion(pred[512,1024]{1,0:T(8,128)(4,1)S(1)} %broadcast_compare_fusion, bf16[512,2,80]{0,2,1:T(8,128)(2,1)} %bitcast.49, bf16[1024,2,80]{0,2,1:T(8,128)(2,1)S(1)} %bitcast.47), kind=kOutput, calls=%fused_computation.4 | convolution fusion | flops 170916864 | bytes 5214208 | tf_op jit(solution)/shard_map/qhd,khd->hqk/dot_general | solution.py:96
  55.2 4.6 %collective-permute-start.8 = (bf16[160,1280]{1,0:T(8,128)(2,1)}, bf16[160,1280]{1,0:T(8,128)(2,1)}, u32[]{:S(2)}, u32[]{:S(2)}) collective-permute-start(bf16[160,1280]{1,0:T(8,128)(2,1)} %collective-permute-done.7), channel_id=1, source_target_pairs={{0,448},{64,0},{128,64},{192,128},{256,192},{320,256},{384,320},{4... | collective-permute-start | bytes 1228808 | tf_op jit(solution)/shard_map/ppermute | solution.py:19
  59.8 3.5 %collective-permute-done.5 = bf16[160,1280]{1,0:T(8,128)(2,1)} collective-permute-done((bf16[160,1280]{1,0:T(8,128)(2,1)S(1)}, bf16[160,1280]{1,0:T(8,128)(2,1)}, u32[]{:S(2)}, u32[]{:S(2)}) %collective-permute-start.5) | collective-permute-done | bytes 409632 | tf_op jit(solution)/shard_map/ppermute | solution.py:17
  63.3 1.9 %collective-permute-start.6 = (bf16[160,1280]{1,0:T(8,128)(2,1)}, bf16[160,1280]{1,0:T(8,128)(2,1)}, u32[]{:S(2)}, u32[]{:S(2)}) collective-permute-start(bf16[160,1280]{1,0:T(8,128)(2,1)} %collective-permute-done.5), channel_id=1, source_target_pairs={{0,64},{64,128},{128,192},{192,256},{256,320},{320,384},{384,448},... | collective-permute-start | bytes 1228808 | tf_op jit(solution)/shard_map/ppermute | solution.py:17
  65.2 1.4 fusion.3
  66.6 1.2 broadcast_in_dim.69
  67.8 4.6 %all-to-all-start = ((bf16[8,512,160]{1,2,0:T(8,128)(2,1)}), bf16[8,512,160]{1,2,0:T(8,128)(2,1)S(1)}, u32[]{:S(2)}, u32[]{:S(2)}) async-start(bf16[8,512,160]{1,2,0:T(8,128)(2,1)} %broadcast_in_dim.69), calls=%async_computation | async-start | bytes 2621440 | tf_op jit(solution)/shard_map/all_to_all | solution.py:107
  72.4 4.7 %collective-permute-start.9 = (bf16[160,1280]{1,0:T(8,128)(2,1)}, bf16[160,1280]{1,0:T(8,128)(2,1)S(1)}, u32[]{:S(2)}, u32[]{:S(2)}) collective-permute-start(bf16[160,1280]{1,0:T(8,128)(2,1)} %collective-permute-done.8), channel_id=1, source_target_pairs={{0,448},{64,0},{128,64},{192,128},{256,192},{320,256},{384,320},{4... | collective-permute-start | bytes 1228808 | tf_op jit(solution)/shard_map/ppermute | solution.py:19
  77.2 1.0 constant_dynamic-update-slice_fusion.15
  78.2 1.0 constant_dynamic-update-slice_fusion.14
  79.3 1.1 constant_dynamic-update-slice_fusion.13
  80.4 1.1 constant_dynamic-update-slice_fusion.12
  81.5 1.0 constant_dynamic-update-slice_fusion.10
  82.5 1.0 constant_dynamic-update-slice_fusion.9
  83.6 25.9 %collective-permute-done.9 = bf16[160,1280]{1,0:T(8,128)(2,1)S(1)} collective-permute-done((bf16[160,1280]{1,0:T(8,128)(2,1)}, bf16[160,1280]{1,0:T(8,128)(2,1)S(1)}, u32[]{:S(2)}, u32[]{:S(2)}) %collective-permute-start.9) | collective-permute-done | bytes 409632 | tf_op jit(solution)/shard_map/ppermute | solution.py:19
  109.5 1.0 constant_dynamic-update-slice_fusion.7
  110.5 1.0 constant_dynamic-update-slice_fusion.6
  111.7 1.0 constant_dynamic-update-slice_fusion.2
  112.7 1.0 constant_dynamic-update-slice_fusion.1
  113.8 2.5 %constant_dynamic-slice_fusion = bf16[1280,1280]{1,0:T(8,128)(2,1)} fusion(bf16[2560,1280]{1,0:T(8,128)(2,1)S(1)} %constant_dynamic-update-slice_fusion, s32[]{:T(128)S(6)} %select_n.174), kind=kLoop, calls=%fused_computation.125 | loop fusion | bytes 6553604 | tf_op jit(solution)/shard_map/jit(_roll_dynamic)/dynamic_slice | solution.py:21
  116.2 4.8 %fusion.42 = (f32[512]{0:T(512)S(1)}, f32[512,1280]{1,0:T(8,128)S(1)}) fusion(f32[512,1280]{1,0:T(8,128)} %copy-done.1, bf16[8,512,160]{1,2,0:T(8,128)(2,1)S(1)} %all-to-all-done, bf16[8,160,1280]{2,1,0:T(8,128)(2,1)} %bitcast.45), kind=kOutput, calls=%fused_computation.130 | convolution fusion | flops 1679031808 | bytes 9832448 | tf_op jit(solution)/shard_map/ztf,zfd->td/dot_general | solution.py:108
  121.1 0.4 multiply_reduce_fusion
  121.5 0.3 multiply_convert_fusion
  121.8 1.7 %reshape.260 = bf16[128,5120]{1,0:T(8,128)(2,1)} reshape(bf16[512,1280]{1,0:T(8,128)(2,1)S(1)} %multiply_convert_fusion) | data formatting | bytes 2621440 | tf_op jit(solution)/shard_map/reshape | solution.py:115
  123.5 1.9 %convolution_convert_fusion.5 = bf16[128,160]{0,1:T(8,128)(2,1)S(1)} fusion(bf16[128,5120]{1,0:T(8,128)(2,1)} %reshape.260, bf16[160,5120]{1,0:T(8,128)(2,1)S(1)} %copy-done), kind=kOutput, calls=%fused_computation.18 | convolution fusion | flops 209735680 | bytes 2990080 | tf_op jit(solution)/shard_map/dot_general | solution.py:45
  125.4 0.1 copy.13
  125.5 0.7 reshape.261
  126.2 13.3 %all-to-all-start.1 = ((bf16[64,2,160]{2,1,0:T(2,128)(2,1)}), bf16[64,2,160]{2,1,0:T(2,128)(2,1)S(1)}, u32[]{:S(2)}, u32[]{:S(2)}) async-start(bf16[64,2,160]{2,1,0:T(2,128)(2,1)} %reshape.261), calls=%async_computation.1 | async-start | bytes 131072 | tf_op jit(solution)/shard_map/all_to_all | solution.py:120
  139.4 0.1 fusion.16
  139.5 9.7 %all-to-all-done.1 = bf16[64,2,160]{2,1,0:T(2,128)(2,1)S(1)} async-done(((bf16[64,2,160]{2,1,0:T(2,128)(2,1)}), bf16[64,2,160]{2,1,0:T(2,128)(2,1)S(1)}, u32[]{:S(2)}, u32[]{:S(2)}) %all-to-all-start.1) | async-done | bytes 40992 | tf_op jit(solution)/shard_map/all_to_all | solution.py:120
  149.2 0.1 reshape.262
  149.3 0.2 convolution_convert_fusion.4
  149.6 0.8 reshape.263
  150.3 4.4 %all-to-all-start.2 = ((bf16[64,4,160]{2,1,0:T(4,128)(2,1)}), bf16[64,4,160]{2,1,0:T(4,128)(2,1)S(1)}, u32[]{:S(2)}, u32[]{:S(2)}) async-start(bf16[64,4,160]{2,1,0:T(4,128)(2,1)} %reshape.263), calls=%async_computation.2 | async-start | bytes 262144 | tf_op jit(solution)/shard_map/all_to_all | solution.py:129
  159.8 5.4 %all-to-all-done.2 = bf16[64,4,160]{2,1,0:T(4,128)(2,1)S(1)} async-done(((bf16[64,4,160]{2,1,0:T(4,128)(2,1)}), bf16[64,4,160]{2,1,0:T(4,128)(2,1)S(1)}, u32[]{:S(2)}, u32[]{:S(2)}) %all-to-all-start.2) | async-done | bytes 81952 | tf_op jit(solution)/shard_map/all_to_all | solution.py:129
  165.3 0.1 reshape.264
  165.3 0.9 convolution_convert_fusion.3
  (43 shorter events, 0.3 us)
Async XLA Ops:
  0.0 123.5 %copy-start = (bf16[160,5120]{1,0:T(8,128)(2,1)S(1)}, bf16[160,5120]{1,0:T(8,128)(2,1)}, u32[]{:S(2)}) copy-start(bf16[160,5120]{1,0:T(8,128)(2,1)} %param.15) | copy-start | bytes 4915204
  0.0 17.2 %copy-start.7 = (bf16[64,1280]{1,0:T(8,128)(2,1)S(1)}, bf16[64,1280]{1,0:T(8,128)(2,1)}, u32[]{:S(2)}) copy-start(bf16[64,1280]{1,0:T(8,128)(2,1)} %param.12) | copy-start | bytes 491524
  0.0 35.7 %collective-permute-start.3 = (bf16[160,1280]{1,0:T(8,128)(2,1)}, bf16[160,1280]{1,0:T(8,128)(2,1)S(1)}, u32[]{:S(2)}, u32[]{:S(2)}) collective-permute-start(bf16[160,1280]{1,0:T(8,128)(2,1)} %param.14), channel_id=1, source_target_pairs={{0,64},{64,128},{128,192},{192,256},{256,320},{320,384},{384,448},... | collective-permute-start | bytes 1228808 | tf_op jit(solution)/shard_map/ppermute | solution.py:17
  5.0 50.2 %collective-permute-start.7 = (bf16[160,1280]{1,0:T(8,128)(2,1)}, bf16[160,1280]{1,0:T(8,128)(2,1)}, u32[]{:S(2)}, u32[]{:S(2)}) collective-permute-start(bf16[160,1280]{1,0:T(8,128)(2,1)} %param.14), channel_id=1, source_target_pairs={{0,448},{64,0},{128,64},{192,128},{256,192},{320,256},{384,320},{4... | collective-permute-start | bytes 1228808 | tf_op jit(solution)/shard_map/ppermute | solution.py:19
  17.8 1.5 copy-start.1
  17.8 2.2 %copy-start.11 = (bf16[3,160,1280]{2,1,0:T(8,128)(2,1)S(1)}, bf16[3,160,1280]{2,1,0:T(8,128)(2,1)}, u32[]{:S(2)}) copy-start(bf16[3,160,1280]{2,1,0:T(8,128)(2,1)} %param.13) | copy-start | bytes 3686404
  18.2 5.9 %copy-start.8 = (s32[512]{0:T(512)S(1)}, s32[512]{0:T(512)}, u32[]{:S(2)}) copy-start(s32[512]{0:T(512)} %param.16) | copy-start | bytes 6148
  18.3 10.9 %copy-start.10 = (s32[64]{0:T(128)S(1)}, s32[64]{0:T(128)}, u32[]{:S(2)}) copy-start(s32[64]{0:T(128)} %param.19) | copy-start | bytes 772
  18.3 11.0 %copy-start.9 = (s32[64]{0:T(128)S(1)}, s32[64]{0:T(128)}, u32[]{:S(2)}) copy-start(s32[64]{0:T(128)} %param.18) | copy-start | bytes 772
  21.3 17.4 %collective-permute-start.2 = (bf16[512,160]{0,1:T(8,128)(2,1)}, bf16[512,160]{0,1:T(8,128)(2,1)}, u32[]{:S(2)}, u32[]{:S(2)}) collective-permute-start(bf16[512,160]{0,1:T(8,128)(2,1)} %convolution_convert_fusion), channel_id=1, source_target_pairs={{0,1},{1,0},{2,3},{3,2},{4,5},{5,4},{6,7},{7,6},{8,9},{9,8},{10,11... | collective-permute-start | bytes 491528 | tf_op jit(solution)/shard_map/ppermute | solution.py:25
  24.2 13.5 %collective-permute-start.1 = (bf16[512]{0:T(512)(128)(2,1)S(1)}, bf16[512]{0:T(512)(128)(2,1)}, u32[]{:S(2)}, u32[]{:S(2)}) collective-permute-start(bf16[512]{0:T(512)(128)(2,1)S(1)} %get-tuple-element.11), channel_id=1, source_target_pairs={{0,1},{1,0},{2,3},{3,2},{4,5},{5,4},{6,7},{7,6},{8,9},{9,8},{10,11... | collective-permute-start | bytes 3080 | tf_op jit(solution)/shard_map/ppermute | solution.py:25
  26.7 25.1 %collective-permute-start = (bf16[512,160]{0,1:T(8,128)(2,1)S(1)}, bf16[512,160]{0,1:T(8,128)(2,1)}, u32[]{:S(2)}, u32[]{:S(2)}) collective-permute-start(bf16[512,160]{0,1:T(8,128)(2,1)S(1)} %convolution_convert_fusion.2), channel_id=1, source_target_pairs={{0,1},{1,0},{2,3},{3,2},{4,5},{5,4},{6,7},{7,6},{8,9},{9,8},{10,11... | collective-permute-start | bytes 491528 | tf_op jit(solution)/shard_map/ppermute | solution.py:25
  35.7 19.5 %copy-start.3 = (bf16[160,1280]{1,0:T(8,128)(2,1)}, bf16[160,1280]{1,0:T(8,128)(2,1)S(1)}, u32[]{:S(2)}) copy-start(bf16[160,1280]{1,0:T(8,128)(2,1)S(1)} %collective-permute-done.3) | copy-start | bytes 1228804
  35.7 14.2 %collective-permute-start.4 = (bf16[160,1280]{1,0:T(8,128)(2,1)S(1)}, bf16[160,1280]{1,0:T(8,128)(2,1)S(1)}, u32[]{:S(2)}, u32[]{:S(2)}) collective-permute-start(bf16[160,1280]{1,0:T(8,128)(2,1)S(1)} %collective-permute-done.3), channel_id=1, source_target_pairs={{0,64},{64,128},{128,192},{192,256},{256,320},{320,384},{384,448},... | collective-permute-start | bytes 1228808 | tf_op jit(solution)/shard_map/ppermute | solution.py:17
  49.9 5.3 %copy-start.5 = (bf16[160,1280]{1,0:T(8,128)(2,1)}, bf16[160,1280]{1,0:T(8,128)(2,1)S(1)}, u32[]{:S(2)}) copy-start(bf16[160,1280]{1,0:T(8,128)(2,1)S(1)} %collective-permute-done.4) | copy-start | bytes 1228804
  49.9 13.4 %collective-permute-start.5 = (bf16[160,1280]{1,0:T(8,128)(2,1)S(1)}, bf16[160,1280]{1,0:T(8,128)(2,1)}, u32[]{:S(2)}, u32[]{:S(2)}) collective-permute-start(bf16[160,1280]{1,0:T(8,128)(2,1)S(1)} %collective-permute-done.4), channel_id=1, source_target_pairs={{0,64},{64,128},{128,192},{192,256},{256,320},{320,384},{384,448},... | collective-permute-start | bytes 1228808 | tf_op jit(solution)/shard_map/ppermute | solution.py:17
  55.2 17.2 %collective-permute-start.8 = (bf16[160,1280]{1,0:T(8,128)(2,1)}, bf16[160,1280]{1,0:T(8,128)(2,1)}, u32[]{:S(2)}, u32[]{:S(2)}) collective-permute-start(bf16[160,1280]{1,0:T(8,128)(2,1)} %collective-permute-done.7), channel_id=1, source_target_pairs={{0,448},{64,0},{128,64},{192,128},{256,192},{320,256},{384,320},{4... | collective-permute-start | bytes 1228808 | tf_op jit(solution)/shard_map/ppermute | solution.py:19
  63.3 13.9 %collective-permute-start.6 = (bf16[160,1280]{1,0:T(8,128)(2,1)}, bf16[160,1280]{1,0:T(8,128)(2,1)}, u32[]{:S(2)}, u32[]{:S(2)}) collective-permute-start(bf16[160,1280]{1,0:T(8,128)(2,1)} %collective-permute-done.5), channel_id=1, source_target_pairs={{0,64},{64,128},{128,192},{192,256},{256,320},{320,384},{384,448},... | collective-permute-start | bytes 1228808 | tf_op jit(solution)/shard_map/ppermute | solution.py:17
  67.8 13.7 %copy-start.2 = (bf16[160,1280]{1,0:T(8,128)(2,1)S(1)}, bf16[160,1280]{1,0:T(8,128)(2,1)}, u32[]{:S(2)}) copy-start(bf16[160,1280]{1,0:T(8,128)(2,1)} %param.14) | copy-start | bytes 1228804
  67.8 48.4 %all-to-all-start = ((bf16[8,512,160]{1,2,0:T(8,128)(2,1)}), bf16[8,512,160]{1,2,0:T(8,128)(2,1)S(1)}, u32[]{:S(2)}, u32[]{:S(2)}) async-start(bf16[8,512,160]{1,2,0:T(8,128)(2,1)} %broadcast_in_dim.69), calls=%async_computation | async-start | bytes 2621440 | tf_op jit(solution)/shard_map/all_to_all | solution.py:107
  72.4 37.0 %collective-permute-start.9 = (bf16[160,1280]{1,0:T(8,128)(2,1)}, bf16[160,1280]{1,0:T(8,128)(2,1)S(1)}, u32[]{:S(2)}, u32[]{:S(2)}) collective-permute-start(bf16[160,1280]{1,0:T(8,128)(2,1)} %collective-permute-done.8), channel_id=1, source_target_pairs={{0,448},{64,0},{128,64},{192,128},{256,192},{320,256},{384,320},{4... | collective-permute-start | bytes 1228808 | tf_op jit(solution)/shard_map/ppermute | solution.py:19
  79.2 32.3 %copy-start.6 = (bf16[160,1280]{1,0:T(8,128)(2,1)S(1)}, bf16[160,1280]{1,0:T(8,128)(2,1)}, u32[]{:S(2)}) copy-start(bf16[160,1280]{1,0:T(8,128)(2,1)} %copy-done.5) | copy-start | bytes 1228804
  80.3 31.2 %copy-start.4 = (bf16[160,1280]{1,0:T(8,128)(2,1)S(1)}, bf16[160,1280]{1,0:T(8,128)(2,1)}, u32[]{:S(2)}) copy-start(bf16[160,1280]{1,0:T(8,128)(2,1)} %copy-done.3) | copy-start | bytes 1228804
  126.2 23.1 %all-to-all-start.1 = ((bf16[64,2,160]{2,1,0:T(2,128)(2,1)}), bf16[64,2,160]{2,1,0:T(2,128)(2,1)S(1)}, u32[]{:S(2)}, u32[]{:S(2)}) async-start(bf16[64,2,160]{2,1,0:T(2,128)(2,1)} %reshape.261), calls=%async_computation.1 | async-start | bytes 131072 | tf_op jit(solution)/shard_map/all_to_all | solution.py:120
  150.3 14.9 %all-to-all-start.2 = ((bf16[64,4,160]{2,1,0:T(4,128)(2,1)}), bf16[64,4,160]{2,1,0:T(4,128)(2,1)S(1)}, u32[]{:S(2)}, u32[]{:S(2)}) async-start(bf16[64,4,160]{2,1,0:T(4,128)(2,1)} %reshape.263), calls=%async_computation.2 | async-start | bytes 262144 | tf_op jit(solution)/shard_map/all_to_all | solution.py:129
